TPU v7x, 32 devices: a whole 2x2x4 slice. The times are simulated.
32 devices in a mesh: section: 4 (over y, x), row: 2 (over core), col: 4 (over z).
Axes of the slice: x: 2, y: 2, z: 4, core: 2. Of those that a mesh axis runs over, the one named last changes fastest.
Arguments:
- cotangent: float32 [4, 128, 4096], P('section', None, ('row', 'col')), may hold values from -6 to 6
- incoming: float32 [4, 128, 4096], P('section', None, ('row', 'col')), may hold values from -6 to 6
- upd_u: float32 [4, 8, 128, 4096], P('section', None, None, ('row', 'col')), may hold values from -4 to 4
- upd_v: float32 [4, 8, 128, 4096], P('section', None, None, ('row', 'col')), may hold values from -0.0078125 to 0.0078125
- saved_x: bfloat16 [4, 4, 128, 4096], P('section', None, None, ('row', 'col')), may hold values from -6 to 6
- saved_h: bfloat16 [4, 4, 2, 128, 14336], P('section', None, None, None, 'col'), may hold values from -6 to 6
- norm_gain: float32 [4, 4096], P('section', ('row', 'col')), may hold values from 0.25 to 1.75
- w_gate: bfloat16 [4, 4096, 14336], P('section', 'row', 'col'), may hold values from -0.09375 to 0.09375
- w_up: bfloat16 [4, 4096, 14336], P('section', 'row', 'col'), may hold values from -0.09375 to 0.09375
- w_down: bfloat16 [4, 14336, 4096], P('section', 'col', 'row'), may hold values from -0.046875 to 0.046875
Outputs:
- new_cotangent: float32 [4, 128, 4096], P('section', None, ('row', 'col'))
- residual_out: float32 [4, 128, 4096], P('section', None, ('row', 'col'))
All inputs are finite; a program needn't handle non-finite values.
Results may differ from a plain program's by a relative error of at most 0.014.
Values may be sent and summed in bfloat16 or wider, within the bound.
No kernel may reach another device: no remote copies, remote signals or barrier semaphores. Data moves between devices by JAX's collectives and lax.ppermute only.
A program may use at most 128 MiB of HBM per device.

v0:
```python
import jax
import jax.numpy as jnp
from jax import lax
from jax.sharding import PartitionSpec as P

D = 4096
eps = 1e-05


def shifted(x, axis, by):
    devices = lax.axis_size(axis)
    return lax.ppermute(x, axis, [(i, (i + by) % devices) for i in range(devices)])


def rotate(carry):
    return shifted(carry, "section", -1)


def shards(cotangent, incoming, upd_u, upd_v, saved_x, saved_h, norm_gain, w_gate, w_up, w_down):
    sections = lax.axis_size("section")
    section_idx = lax.axis_index("section")
    inputs_all = saved_x[0].astype(jnp.float32)
    hidden_all = saved_h[0]
    gain = norm_gain[0]
    wg = w_gate[0]
    wu = w_up[0]
    wd = w_down[0]

    def layer_step(step, carry):
        carry = rotate(carry)
        micro = (section_idx + step + 1) % sections
        xf = lax.dynamic_index_in_dim(inputs_all, micro, 0, keepdims=False)
        hpair = lax.dynamic_index_in_dim(hidden_all, micro, 0, keepdims=False)
        sumsq = lax.psum(jnp.sum(xf * xf, axis=1), ("row", "col"))
        gy = carry.astype(jnp.bfloat16)
        wide = lax.all_gather(gy, "col", axis=1, tiled=True)
        ga_part = lax.dot_general(
            wide, wd, (((1,), (1,)), ((), ())), preferred_element_type=jnp.float32
        )
        ga = lax.psum_scatter(ga_part, "row", scatter_dimension=1, tiled=True)
        width = ga.shape[1]
        offset = lax.axis_index("row") * width
        hg = lax.dynamic_slice_in_dim(hpair[0], offset, width, 1).astype(jnp.float32)
        hu = lax.dynamic_slice_in_dim(hpair[1], offset, width, 1).astype(jnp.float32)
        sig = jax.nn.sigmoid(hg)
        part_gate = (ga * hu * sig * (1.0 + hg * (1.0 - sig))).astype(jnp.bfloat16)
        part_up = (ga * hg * sig).astype(jnp.bfloat16)
        grad_gate, grad_up = (
            lax.all_gather(part_gate, "row", axis=1, tiled=True),
            lax.all_gather(part_up, "row", axis=1, tiled=True),
        )
        first = lax.dot_general(
            wg, grad_gate, (((1,), (1,)), ((), ())), preferred_element_type=jnp.float32
        )
        second = lax.dot_general(
            wu, grad_up, (((1,), (1,)), ((), ())), preferred_element_type=jnp.float32
        )
        normgrad = lax.psum_scatter(first + second, "col", scatter_dimension=0, tiled=True).T
        rstd = lax.rsqrt(sumsq / D + eps)[:, None]
        scaled = gain * normgrad
        inner = lax.psum(jnp.sum(scaled * xf, axis=1), ("row", "col"))[:, None] / D
        updated = carry + rstd * scaled - xf * (rstd * rstd * rstd) * inner
        active = jnp.logical_and(step >= micro, step - micro < sections)
        return jnp.where(active, updated, carry)

    pulled = lax.fori_loop(0, 2 * sections - 1, layer_step, cotangent[0])
    pulled = rotate(pulled)
    resid = pulled + incoming[0] - cotangent[0]
    local_dots = jnp.einsum("urd,rd->u", upd_v[0], resid, precision=lax.Precision.HIGHEST)
    dots = lax.psum(local_dots, ("row", "col"))
    update = jnp.einsum("u,urd->rd", dots, upd_u[0], precision=lax.Precision.HIGHEST)
    fresh = cotangent[0] + resid - update
    return (fresh[None], resid[None])


def solution(mesh):
    placed = (
        P("section", None, ("row", "col")),
        P("section", None, ("row", "col")),
        P("section", None, None, ("row", "col")),
        P("section", None, None, ("row", "col")),
        P("section", None, None, ("row", "col")),
        P("section", None, None, None, "col"),
        P("section", ("row", "col")),
        P("section", "row", "col"),
        P("section", "row", "col"),
        P("section", "col", "row"),
    )
    return jax.shard_map(
        shards,
        mesh=mesh,
        in_specs=placed,
        out_specs=(P("section", None, ("row", "col")), P("section", None, ("row", "col"))),
        check_vma=False,
    )
```

profile of v0, /device:TPU:0, one launch (start us, length us, event | category | flops | bytes accessed | tf_op | source)
XLA Modules:
  0.0 880.5 jit_solution(12553855589407518897)
XLA Ops:
  10.2 832.8 %while.15 = (s32[]{:T(128)}, f32[128,512]{1,0:T(8,128)}, s32[]{:T(128)}, f32[4,128,512]{2,1,0:T(8,128)S(1)}, f32[1,512]{1,0:T(1,128)}, /*index=5*/bf16[3584,2048...) while((s32[]{:T(128)}, f32[128,512]{1,0:T(8,128)}, ...), condition=%wide.region_7.8_spmd, body=%wide.region_0.7_spmd.sunk | while | flops 5641699840 | bytes 72765032 | solution.py:66
  20.1 15.1 %all_gather.33 = bf16[128,2048]{1,0:T(8,128)(2,1)S(1)} all-gather(bf16[128,512]{1,0:T(8,128)(2,1)S(1)} %convert_element_type.72), channel_id=1, replica_groups=mesh['section'=4,'row'=2,'col'=4] {'col'}, dimensions={1}, use_global_device_ids=true | all-gather | bytes 655360 | tf_op jit(solution)/shard_map/while/body/eval_jaxpr/all_gather | solution.py:36
  46.7 12.0 %reduce-scatter.3.cloned.1.call-done = f32[128,1792]{1,0:T(8,128)} async-done(((f32[128,3584]{1,0:T(8,128)}), f32[128,1792]{1,0:T(8,128)}) %reduce-scatter.3.cloned.1.call-update) | async-done | bytes 917520 | tf_op jit(solution)/shard_map/while/body/eval_jaxpr/reduce_scatter | solution.py:40
  86.4 28.7 %reduce-scatter.5.cloned.1.call-done = f32[512,128]{0,1:T(8,128)} async-done(((f32[2048,128]{0,1:T(8,128)}), f32[512,128]{0,1:T(8,128)}) %reduce-scatter.5.cloned.1.call-update) | async-done | bytes 262160 | tf_op jit(solution)/shard_map/while/body/eval_jaxpr/reduce_scatter | solution.py:58
  116.2 13.7 %all-reduce.2 = (f32[128]{0:T(128)S(1)}, f32[128]{0:T(128)S(1)}) all-reduce(f32[128]{0:T(128)S(1)} %get-tuple-element.317, f32[128]{0:T(128)S(1)} %get-tuple-element.318), channel_id=1, replica_groups=mesh['section'=4,'row'=2,'col'=4] {'row','col'}, use_global_device_ids=true, to_apply=%region_6.6 | all-reduce | flops 256 | bytes 2048 | tf_op jit(solution)/shard_map/while/body/eval_jaxpr/psum | solution.py:61
  141.1 16.1 %all_gather.33 = bf16[128,2048]{1,0:T(8,128)(2,1)S(1)} all-gather(bf16[128,512]{1,0:T(8,128)(2,1)S(1)} %convert_element_type.72), channel_id=1, replica_groups=mesh['section'=4,'row'=2,'col'=4] {'col'}, dimensions={1}, use_global_device_ids=true | all-gather | bytes 655360 | tf_op jit(solution)/shard_map/while/body/eval_jaxpr/all_gather | solution.py:36
  205.0 28.7 %reduce-scatter.5.cloned.1.call-done = f32[512,128]{0,1:T(8,128)} async-done(((f32[2048,128]{0,1:T(8,128)}), f32[512,128]{0,1:T(8,128)}) %reduce-scatter.5.cloned.1.call-update) | async-done | bytes 262160 | tf_op jit(solution)/shard_map/while/body/eval_jaxpr/reduce_scatter | solution.py:58
  234.8 13.7 %all-reduce.2 = (f32[128]{0:T(128)S(1)}, f32[128]{0:T(128)S(1)}) all-reduce(f32[128]{0:T(128)S(1)} %get-tuple-element.317, f32[128]{0:T(128)S(1)} %get-tuple-element.318), channel_id=1, replica_groups=mesh['section'=4,'row'=2,'col'=4] {'row','col'}, use_global_device_ids=true, to_apply=%region_6.6 | all-reduce | flops 256 | bytes 2048 | tf_op jit(solution)/shard_map/while/body/eval_jaxpr/psum | solution.py:61
  259.7 16.2 %all_gather.33 = bf16[128,2048]{1,0:T(8,128)(2,1)S(1)} all-gather(bf16[128,512]{1,0:T(8,128)(2,1)S(1)} %convert_element_type.72), channel_id=1, replica_groups=mesh['section'=4,'row'=2,'col'=4] {'col'}, dimensions={1}, use_global_device_ids=true | all-gather | bytes 655360 | tf_op jit(solution)/shard_map/while/body/eval_jaxpr/all_gather | solution.py:36
  323.5 28.7 %reduce-scatter.5.cloned.1.call-done = f32[512,128]{0,1:T(8,128)} async-done(((f32[2048,128]{0,1:T(8,128)}), f32[512,128]{0,1:T(8,128)}) %reduce-scatter.5.cloned.1.call-update) | async-done | bytes 262160 | tf_op jit(solution)/shard_map/while/body/eval_jaxpr/reduce_scatter | solution.py:58
  353.3 13.7 %all-reduce.2 = (f32[128]{0:T(128)S(1)}, f32[128]{0:T(128)S(1)}) all-reduce(f32[128]{0:T(128)S(1)} %get-tuple-element.317, f32[128]{0:T(128)S(1)} %get-tuple-element.318), channel_id=1, replica_groups=mesh['section'=4,'row'=2,'col'=4] {'row','col'}, use_global_device_ids=true, to_apply=%region_6.6 | all-reduce | flops 256 | bytes 2048 | tf_op jit(solution)/shard_map/while/body/eval_jaxpr/psum | solution.py:61
  378.2 16.2 %all_gather.33 = bf16[128,2048]{1,0:T(8,128)(2,1)S(1)} all-gather(bf16[128,512]{1,0:T(8,128)(2,1)S(1)} %convert_element_type.72), channel_id=1, replica_groups=mesh['section'=4,'row'=2,'col'=4] {'col'}, dimensions={1}, use_global_device_ids=true | all-gather | bytes 655360 | tf_op jit(solution)/shard_map/while/body/eval_jaxpr/all_gather | solution.py:36
  442.0 28.7 %reduce-scatter.5.cloned.1.call-done = f32[512,128]{0,1:T(8,128)} async-done(((f32[2048,128]{0,1:T(8,128)}), f32[512,128]{0,1:T(8,128)}) %reduce-scatter.5.cloned.1.call-update) | async-done | bytes 262160 | tf_op jit(solution)/shard_map/while/body/eval_jaxpr/reduce_scatter | solution.py:58
  471.8 13.7 %all-reduce.2 = (f32[128]{0:T(128)S(1)}, f32[128]{0:T(128)S(1)}) all-reduce(f32[128]{0:T(128)S(1)} %get-tuple-element.317, f32[128]{0:T(128)S(1)} %get-tuple-element.318), channel_id=1, replica_groups=mesh['section'=4,'row'=2,'col'=4] {'row','col'}, use_global_device_ids=true, to_apply=%region_6.6 | all-reduce | flops 256 | bytes 2048 | tf_op jit(solution)/shard_map/while/body/eval_jaxpr/psum | solution.py:61
  496.7 16.2 %all_gather.33 = bf16[128,2048]{1,0:T(8,128)(2,1)S(1)} all-gather(bf16[128,512]{1,0:T(8,128)(2,1)S(1)} %convert_element_type.72), channel_id=1, replica_groups=mesh['section'=4,'row'=2,'col'=4] {'col'}, dimensions={1}, use_global_device_ids=true | all-gather | bytes 655360 | tf_op jit(solution)/shard_map/while/body/eval_jaxpr/all_gather | solution.py:36
  560.6 28.7 %reduce-scatter.5.cloned.1.call-done = f32[512,128]{0,1:T(8,128)} async-done(((f32[2048,128]{0,1:T(8,128)}), f32[512,128]{0,1:T(8,128)}) %reduce-scatter.5.cloned.1.call-update) | async-done | bytes 262160 | tf_op jit(solution)/shard_map/while/body/eval_jaxpr/reduce_scatter | solution.py:58
  590.4 13.7 %all-reduce.2 = (f32[128]{0:T(128)S(1)}, f32[128]{0:T(128)S(1)}) all-reduce(f32[128]{0:T(128)S(1)} %get-tuple-element.317, f32[128]{0:T(128)S(1)} %get-tuple-element.318), channel_id=1, replica_groups=mesh['section'=4,'row'=2,'col'=4] {'row','col'}, use_global_device_ids=true, to_apply=%region_6.6 | all-reduce | flops 256 | bytes 2048 | tf_op jit(solution)/shard_map/while/body/eval_jaxpr/psum | solution.py:61
  615.3 16.2 %all_gather.33 = bf16[128,2048]{1,0:T(8,128)(2,1)S(1)} all-gather(bf16[128,512]{1,0:T(8,128)(2,1)S(1)} %convert_element_type.72), channel_id=1, replica_groups=mesh['section'=4,'row'=2,'col'=4] {'col'}, dimensions={1}, use_global_device_ids=true | all-gather | bytes 655360 | tf_op jit(solution)/shard_map/while/body/eval_jaxpr/all_gather | solution.py:36
  679.1 28.7 %reduce-scatter.5.cloned.1.call-done = f32[512,128]{0,1:T(8,128)} async-done(((f32[2048,128]{0,1:T(8,128)}), f32[512,128]{0,1:T(8,128)}) %reduce-scatter.5.cloned.1.call-update) | async-done | bytes 262160 | tf_op jit(solution)/shard_map/while/body/eval_jaxpr/reduce_scatter | solution.py:58
  708.9 13.7 %all-reduce.2 = (f32[128]{0:T(128)S(1)}, f32[128]{0:T(128)S(1)}) all-reduce(f32[128]{0:T(128)S(1)} %get-tuple-element.317, f32[128]{0:T(128)S(1)} %get-tuple-element.318), channel_id=1, replica_groups=mesh['section'=4,'row'=2,'col'=4] {'row','col'}, use_global_device_ids=true, to_apply=%region_6.6 | all-reduce | flops 256 | bytes 2048 | tf_op jit(solution)/shard_map/while/body/eval_jaxpr/psum | solution.py:61
  733.8 16.2 %all_gather.33 = bf16[128,2048]{1,0:T(8,128)(2,1)S(1)} all-gather(bf16[128,512]{1,0:T(8,128)(2,1)S(1)} %convert_element_type.72), channel_id=1, replica_groups=mesh['section'=4,'row'=2,'col'=4] {'col'}, dimensions={1}, use_global_device_ids=true | all-gather | bytes 655360 | tf_op jit(solution)/shard_map/while/body/eval_jaxpr/all_gather | solution.py:36
  797.6 28.7 %reduce-scatter.5.cloned.1.call-done = f32[512,128]{0,1:T(8,128)} async-done(((f32[2048,128]{0,1:T(8,128)}), f32[512,128]{0,1:T(8,128)}) %reduce-scatter.5.cloned.1.call-update) | async-done | bytes 262160 | tf_op jit(solution)/shard_map/while/body/eval_jaxpr/reduce_scatter | solution.py:58
  827.4 13.7 %all-reduce.2 = (f32[128]{0:T(128)S(1)}, f32[128]{0:T(128)S(1)}) all-reduce(f32[128]{0:T(128)S(1)} %get-tuple-element.317, f32[128]{0:T(128)S(1)} %get-tuple-element.318), channel_id=1, replica_groups=mesh['section'=4,'row'=2,'col'=4] {'row','col'}, use_global_device_ids=true, to_apply=%region_6.6 | all-reduce | flops 256 | bytes 2048 | tf_op jit(solution)/shard_map/while/body/eval_jaxpr/psum | solution.py:61
  855.4 14.0 %psum.35 = f32[8]{0:T(128)S(1)} all-reduce(f32[8]{0:T(128)S(1)} %fusion.16), channel_id=1, replica_groups=mesh['section'=4,'row'=2,'col'=4] {'row','col'}, use_global_device_ids=true, to_apply=%region_8.9 | all-reduce | flops 8 | bytes 64 | tf_op jit(solution)/shard_map/psum | solution.py:70
  (144 shorter events, 431.0 us)
Async XLA Ops:
  7.2 862.2 %copy-start = (f32[1,8,128,512]{3,2,1,0:T(8,128)S(1)}, f32[1,8,128,512]{3,2,1,0:T(8,128)}, u32[]{:S(2)}) copy-start(f32[1,8,128,512]{3,2,1,0:T(8,128)} %param.14) | copy-start | bytes 6291460
  10.2 48.5 %reduce-scatter.3.cloned.1.call-start = ((), (), s32[]{:S(2)}) async-start(), calls=%async_computation.2 | async-start | bytes 2752512 | tf_op jit(solution)/shard_map/while/body/eval_jaxpr/reduce_scatter | solution.py:40
  10.2 9.9 %collective-permute-start = (f32[128,512]{1,0:T(8,128)}, f32[128,512]{1,0:T(8,128)S(1)}, u32[]{:S(2)}, u32[]{:S(2)}) collective-permute-start(f32[128,512]{1,0:T(8,128)} %get-tuple-element.343), channel_id=1, source_target_pairs={{0,24},{8,0},{16,8},{24,16},{1,25},{9,1},{17,9},{25,17},{2,26},{10... | collective-permute-start | bytes 786440 | tf_op jit(solution)/shard_map/while/body/eval_jaxpr/ppermute | solution.py:12
  46.6 68.5 %reduce-scatter.5.cloned.1.call-start = ((), (), s32[]{:S(2)}) async-start(), calls=%async_computation.3 | async-start | bytes 1310720 | tf_op jit(solution)/shard_map/while/body/eval_jaxpr/reduce_scatter | solution.py:58
  131.7 45.6 %reduce-scatter.3.cloned.1.call-start = ((), (), s32[]{:S(2)}) async-start(), calls=%async_computation.2 | async-start | bytes 2752512 | tf_op jit(solution)/shard_map/while/body/eval_jaxpr/reduce_scatter | solution.py:40
  131.7 9.4 %collective-permute-start = (f32[128,512]{1,0:T(8,128)}, f32[128,512]{1,0:T(8,128)S(1)}, u32[]{:S(2)}, u32[]{:S(2)}) collective-permute-start(f32[128,512]{1,0:T(8,128)} %get-tuple-element.343), channel_id=1, source_target_pairs={{0,24},{8,0},{16,8},{24,16},{1,25},{9,1},{17,9},{25,17},{2,26},{10... | collective-permute-start | bytes 786440 | tf_op jit(solution)/shard_map/while/body/eval_jaxpr/ppermute | solution.py:12
  168.6 65.1 %reduce-scatter.5.cloned.1.call-start = ((), (), s32[]{:S(2)}) async-start(), calls=%async_computation.3 | async-start | bytes 1310720 | tf_op jit(solution)/shard_map/while/body/eval_jaxpr/reduce_scatter | solution.py:58
  194.0 39.7 %copy-start.2 = (f32[1,512]{1,0:T(1,128)S(1)}, f32[1,512]{1,0:T(1,128)}, u32[]{:S(2)}) copy-start(f32[1,512]{1,0:T(1,128)} %get-tuple-element.364) | copy-start | bytes 6148 | tf_op jit(solution)/shard_map/while
  250.3 45.6 %reduce-scatter.3.cloned.1.call-start = ((), (), s32[]{:S(2)}) async-start(), calls=%async_computation.2 | async-start | bytes 2752512 | tf_op jit(solution)/shard_map/while/body/eval_jaxpr/reduce_scatter | solution.py:40
  250.3 9.4 %collective-permute-start = (f32[128,512]{1,0:T(8,128)}, f32[128,512]{1,0:T(8,128)S(1)}, u32[]{:S(2)}, u32[]{:S(2)}) collective-permute-start(f32[128,512]{1,0:T(8,128)} %get-tuple-element.343), channel_id=1, source_target_pairs={{0,24},{8,0},{16,8},{24,16},{1,25},{9,1},{17,9},{25,17},{2,26},{10... | collective-permute-start | bytes 786440 | tf_op jit(solution)/shard_map/while/body/eval_jaxpr/ppermute | solution.py:12
  287.2 65.0 %reduce-scatter.5.cloned.1.call-start = ((), (), s32[]{:S(2)}) async-start(), calls=%async_computation.3 | async-start | bytes 1310720 | tf_op jit(solution)/shard_map/while/body/eval_jaxpr/reduce_scatter | solution.py:58
  368.8 45.5 %reduce-scatter.3.cloned.1.call-start = ((), (), s32[]{:S(2)}) async-start(), calls=%async_computation.2 | async-start | bytes 2752512 | tf_op jit(solution)/shard_map/while/body/eval_jaxpr/reduce_scatter | solution.py:40
  368.8 9.4 %collective-permute-start = (f32[128,512]{1,0:T(8,128)}, f32[128,512]{1,0:T(8,128)S(1)}, u32[]{:S(2)}, u32[]{:S(2)}) collective-permute-start(f32[128,512]{1,0:T(8,128)} %get-tuple-element.343), channel_id=1, source_target_pairs={{0,24},{8,0},{16,8},{24,16},{1,25},{9,1},{17,9},{25,17},{2,26},{10... | collective-permute-start | bytes 786440 | tf_op jit(solution)/shard_map/while/body/eval_jaxpr/ppermute | solution.py:12
  405.8 65.0 %reduce-scatter.5.cloned.1.call-start = ((), (), s32[]{:S(2)}) async-start(), calls=%async_computation.3 | async-start | bytes 1310720 | tf_op jit(solution)/shard_map/while/body/eval_jaxpr/reduce_scatter | solution.py:58
  487.4 45.5 %reduce-scatter.3.cloned.1.call-start = ((), (), s32[]{:S(2)}) async-start(), calls=%async_computation.2 | async-start | bytes 2752512 | tf_op jit(solution)/shard_map/while/body/eval_jaxpr/reduce_scatter | solution.py:40
  487.4 9.4 %collective-permute-start = (f32[128,512]{1,0:T(8,128)}, f32[128,512]{1,0:T(8,128)S(1)}, u32[]{:S(2)}, u32[]{:S(2)}) collective-permute-start(f32[128,512]{1,0:T(8,128)} %get-tuple-element.343), channel_id=1, source_target_pairs={{0,24},{8,0},{16,8},{24,16},{1,25},{9,1},{17,9},{25,17},{2,26},{10... | collective-permute-start | bytes 786440 | tf_op jit(solution)/shard_map/while/body/eval_jaxpr/ppermute | solution.py:12
  524.3 65.0 %reduce-scatter.5.cloned.1.call-start = ((), (), s32[]{:S(2)}) async-start(), calls=%async_computation.3 | async-start | bytes 1310720 | tf_op jit(solution)/shard_map/while/body/eval_jaxpr/reduce_scatter | solution.py:58
  605.9 45.5 %reduce-scatter.3.cloned.1.call-start = ((), (), s32[]{:S(2)}) async-start(), calls=%async_computation.2 | async-start | bytes 2752512 | tf_op jit(solution)/shard_map/while/body/eval_jaxpr/reduce_scatter | solution.py:40
  605.9 9.4 %collective-permute-start = (f32[128,512]{1,0:T(8,128)}, f32[128,512]{1,0:T(8,128)S(1)}, u32[]{:S(2)}, u32[]{:S(2)}) collective-permute-start(f32[128,512]{1,0:T(8,128)} %get-tuple-element.343), channel_id=1, source_target_pairs={{0,24},{8,0},{16,8},{24,16},{1,25},{9,1},{17,9},{25,17},{2,26},{10... | collective-permute-start | bytes 786440 | tf_op jit(solution)/shard_map/while/body/eval_jaxpr/ppermute | solution.py:12
  642.8 65.0 %reduce-scatter.5.cloned.1.call-start = ((), (), s32[]{:S(2)}) async-start(), calls=%async_computation.3 | async-start | bytes 1310720 | tf_op jit(solution)/shard_map/while/body/eval_jaxpr/reduce_scatter | solution.py:58
  724.4 45.5 %reduce-scatter.3.cloned.1.call-start = ((), (), s32[]{:S(2)}) async-start(), calls=%async_computation.2 | async-start | bytes 2752512 | tf_op jit(solution)/shard_map/while/body/eval_jaxpr/reduce_scatter | solution.py:40
  724.4 9.4 %collective-permute-start = (f32[128,512]{1,0:T(8,128)}, f32[128,512]{1,0:T(8,128)S(1)}, u32[]{:S(2)}, u32[]{:S(2)}) collective-permute-start(f32[128,512]{1,0:T(8,128)} %get-tuple-element.343), channel_id=1, source_target_pairs={{0,24},{8,0},{16,8},{24,16},{1,25},{9,1},{17,9},{25,17},{2,26},{10... | collective-permute-start | bytes 786440 | tf_op jit(solution)/shard_map/while/body/eval_jaxpr/ppermute | solution.py:12
  761.3 65.0 %reduce-scatter.5.cloned.1.call-start = ((), (), s32[]{:S(2)}) async-start(), calls=%async_computation.3 | async-start | bytes 1310720 | tf_op jit(solution)/shard_map/while/body/eval_jaxpr/reduce_scatter | solution.py:58
  842.9 9.4 %collective-permute-start.1 = (f32[128,512]{1,0:T(8,128)}, f32[128,512]{1,0:T(8,128)S(1)}, u32[]{:S(2)}, u32[]{:S(2)}) collective-permute-start(f32[128,512]{1,0:T(8,128)} %get-tuple-element.223), channel_id=1, source_target_pairs={{0,24},{8,0},{16,8},{24,16},{1,25},{9,1},{17,9},{25,17},{2,26},{10... | collective-permute-start | bytes 786440 | tf_op jit(solution)/shard_map/ppermute | solution.py:12
  (7 other events, 258.8 us)
Sparse Core Ops, SparseCore 0:
  46.7 11.8 reduce-scatter.2
  86.5 28.5 reduce-scatter.4
  168.7 8.5 reduce-scatter.2
  205.1 28.5 reduce-scatter.4
  287.3 8.4 reduce-scatter.2
  323.6 28.5 reduce-scatter.4
  405.9 8.4 reduce-scatter.2
  442.2 28.5 reduce-scatter.4
  524.4 8.4 reduce-scatter.2
  560.7 28.5 reduce-scatter.4
  642.9 8.4 reduce-scatter.2
  679.2 28.5 reduce-scatter.4
  761.5 8.4 reduce-scatter.2
  797.7 28.5 reduce-scatter.4
where the time goes:
time: 882 us; the launch traced here: 881 us
  waiting for transfers between devices  319 us (36%)
  blocking collectives  256 us (29%)
  matrix products  228 us (26%)
  other arithmetic  39.4 us (4%)
  starting transfers between devices  21 us (2%)
  between operations  13.7 us (2%)
    reduce_scatter x7, waiting for transfers between devices, layer_step(): lax.psum_scatter(first + second, 'col', scatter_dimension=0, tiled=True)  201 us
    all_gather x7, blocking collectives, layer_step(): wide = lax.all_gather(gy, 'col', axis=1, tiled=True)  112 us
    psum x7, blocking collectives, layer_step(): inner = lax.psum(jnp.sum(scaled * xf, axis=1), ('row', 'col'))[:, None] / D  95.9 us
    dot_general x7, matrix products, layer_step(): lax.dot_general(wide, wd, (((1,), (1,)), ((), ())), preferred_element_typ...  79.4 us
    dot_general x7, matrix products, layer_step(): lax.dot_general(wu, grad_up, (((1,), (1,)), ((), ())), preferred_element_...  76.5 us
    dot_general x7, matrix products, layer_step(): lax.dot_general(wg, grad_gate, (((1,), (1,)), ((), ())), preferred_elemen...  69.4 us
    reduce_scatter x7, waiting for transfers between devices, layer_step(): ga = lax.psum_scatter(ga_part, 'row', scatter_dimension=1, tiled=True)  63.1 us
    ppermute x8, waiting for transfers between devices, shifted(): lax.ppermute(x, axis, [(i, (i + by) % devices) for i in range(devices)])  54.8 us
  transfers between devices with their start and end apart: 22, of which 22 were waited for; matrix products, arithmetic and copies ran while one was open for 0% of the time, Pallas kernels for 0%

commit v1 on v0

--- a/solution.py
+++ b/solution.py
@@ -58,7 +58,12 @@
         normgrad = lax.psum_scatter(first + second, "col", scatter_dimension=0, tiled=True).T
         rstd = lax.rsqrt(sumsq / D + eps)[:, None]
         scaled = gain * normgrad
-        inner = lax.psum(jnp.sum(scaled * xf, axis=1), ("row", "col"))[:, None] / D
+        inner = (
+            jnp.sum(lax.all_gather(jnp.sum(scaled * xf, axis=1), axis_name=("row", "col")), 0)[
+                :, None
+            ]
+            / D
+        )
         updated = carry + rstd * scaled - xf * (rstd * rstd * rstd) * inner
         active = jnp.logical_and(step >= micro, step - micro < sections)
         return jnp.where(active, updated, carry)

time: 882 us -> 980 us (1.11)
  blocking collectives: 256 us -> 359 us
    all_gather x0 -> x7, blocking collectives: none -> 89.5 us  [layer_step(): lax.all_gather(jnp.sum(scaled * xf, axis=1), axis_name=('row', 'col'))]
    psum x7, blocking collectives: 95.9 us -> 112 us  [layer_step(): sumsq = lax.psum(jnp.sum(xf * xf, axis=1), ('row', 'col'))]
where the time goes in v1:
time: 980 us; the launch traced here: 978 us
  blocking collectives  359 us (37%)
  waiting for transfers between devices  314 us (32%)
  matrix products  228 us (23%)
  other arithmetic  39.7 us (4%)
  starting transfers between devices  21 us (2%)
  between operations  13.7 us (1%)
    reduce_scatter x7, waiting for transfers between devices, layer_step(): lax.psum_scatter(first + second, 'col', scatter_dimension=0, tiled=True)  201 us
    psum x7, blocking collectives, layer_step(): sumsq = lax.psum(jnp.sum(xf * xf, axis=1), ('row', 'col'))  112 us
    all_gather x7, blocking collectives, layer_step(): wide = lax.all_gather(gy, 'col', axis=1, tiled=True)  110 us
    all_gather x7, blocking collectives, layer_step(): lax.all_gather(jnp.sum(scaled * xf, axis=1), axis_name=('row', 'col'))  89.5 us
    dot_general x7, matrix products, layer_step(): lax.dot_general(wide, wd, (((1,), (1,)), ((), ())), preferred_element_typ...  79.4 us
    dot_general x7, matrix products, layer_step(): lax.dot_general(wu, grad_up, (((1,), (1,)), ((), ())), preferred_element_...  76.5 us
    dot_general x7, matrix products, layer_step(): lax.dot_general(wg, grad_gate, (((1,), (1,)), ((), ())), preferred_elemen...  69.4 us
    reduce_scatter x7, waiting for transfers between devices, layer_step(): ga = lax.psum_scatter(ga_part, 'row', scatter_dimension=1, tiled=True)  63.6 us
  transfers between devices with their start and end apart: 22, of which 22 were waited for; matrix products, arithmetic and copies ran while one was open for 0% of the time, Pallas kernels for 0%

profile of v1, /device:TPU:0, one launch (start us, length us, event | category | flops | bytes accessed | tf_op | source)
XLA Modules:
  0.0 978.1 jit_solution(1088504964399017799)
XLA Ops:
  10.2 931.3 %while.15 = (s32[]{:T(128)}, f32[128,512]{1,0:T(8,128)}, s32[]{:T(128)}, f32[4,128,512]{2,1,0:T(8,128)S(1)}, f32[1,512]{1,0:T(1,128)}, /*index=5*/bf16[3584,2048...) while((s32[]{:T(128)}, f32[128,512]{1,0:T(8,128)}, ...), condition=%wide.region_7.8_spmd, body=%wide.region_0.7_spmd.sunk | while | flops 5641700864 | bytes 72773232 | solution.py:71
  20.1 15.1 %all_gather.53 = bf16[128,2048]{1,0:T(8,128)(2,1)S(1)} all-gather(bf16[128,512]{1,0:T(8,128)(2,1)S(1)} %convert_element_type.72), channel_id=1, replica_groups=mesh['section'=4,'row'=2,'col'=4] {'col'}, dimensions={1}, use_global_device_ids=true | all-gather | bytes 655360 | tf_op jit(solution)/shard_map/while/body/eval_jaxpr/all_gather | solution.py:36
  86.4 28.7 %reduce-scatter.5.cloned.1.call-done = f32[512,128]{0,1:T(8,128)} async-done(((f32[2048,128]{0,1:T(8,128)}), f32[512,128]{0,1:T(8,128)}) %reduce-scatter.5.cloned.1.call-update) | async-done | bytes 262160 | tf_op jit(solution)/shard_map/while/body/eval_jaxpr/reduce_scatter | solution.py:58
  116.2 12.8 %all-gather.3 = f32[8,1,128]{2,1,0:T(1,128)S(1)} all-gather(f32[1,1,128]{2,1,0:T(1,128)S(1)} %bitcast.111), channel_id=2, replica_groups=mesh['section'=4,'row'=2,'col'=4] {'row','col'}, dimensions={0}, use_global_device_ids=true | all-gather | bytes 4608 | tf_op jit(solution)/shard_map/while/body/eval_jaxpr/all_gather | solution.py:62
  129.0 15.9 %psum.23 = f32[128]{0:T(128)S(1)} all-reduce(f32[128]{0:T(128)S(1)} %get-tuple-element.312), channel_id=1, replica_groups=mesh['section'=4,'row'=2,'col'=4] {'row','col'}, use_global_device_ids=true, to_apply=%region_2.2 | all-reduce | flops 128 | bytes 1024 | tf_op jit(solution)/shard_map/while/body/eval_jaxpr/psum | solution.py:34
  155.3 15.8 %all_gather.53 = bf16[128,2048]{1,0:T(8,128)(2,1)S(1)} all-gather(bf16[128,512]{1,0:T(8,128)(2,1)S(1)} %convert_element_type.72), channel_id=1, replica_groups=mesh['section'=4,'row'=2,'col'=4] {'col'}, dimensions={1}, use_global_device_ids=true | all-gather | bytes 655360 | tf_op jit(solution)/shard_map/while/body/eval_jaxpr/all_gather | solution.py:36
  218.9 28.7 %reduce-scatter.5.cloned.1.call-done = f32[512,128]{0,1:T(8,128)} async-done(((f32[2048,128]{0,1:T(8,128)}), f32[512,128]{0,1:T(8,128)}) %reduce-scatter.5.cloned.1.call-update) | async-done | bytes 262160 | tf_op jit(solution)/shard_map/while/body/eval_jaxpr/reduce_scatter | solution.py:58
  261.5 15.9 %psum.23 = f32[128]{0:T(128)S(1)} all-reduce(f32[128]{0:T(128)S(1)} %get-tuple-element.312), channel_id=1, replica_groups=mesh['section'=4,'row'=2,'col'=4] {'row','col'}, use_global_device_ids=true, to_apply=%region_2.2 | all-reduce | flops 128 | bytes 1024 | tf_op jit(solution)/shard_map/while/body/eval_jaxpr/psum | solution.py:34
  287.8 15.8 %all_gather.53 = bf16[128,2048]{1,0:T(8,128)(2,1)S(1)} all-gather(bf16[128,512]{1,0:T(8,128)(2,1)S(1)} %convert_element_type.72), channel_id=1, replica_groups=mesh['section'=4,'row'=2,'col'=4] {'col'}, dimensions={1}, use_global_device_ids=true | all-gather | bytes 655360 | tf_op jit(solution)/shard_map/while/body/eval_jaxpr/all_gather | solution.py:36
  351.3 28.7 %reduce-scatter.5.cloned.1.call-done = f32[512,128]{0,1:T(8,128)} async-done(((f32[2048,128]{0,1:T(8,128)}), f32[512,128]{0,1:T(8,128)}) %reduce-scatter.5.cloned.1.call-update) | async-done | bytes 262160 | tf_op jit(solution)/shard_map/while/body/eval_jaxpr/reduce_scatter | solution.py:58
  393.9 15.9 %psum.23 = f32[128]{0:T(128)S(1)} all-reduce(f32[128]{0:T(128)S(1)} %get-tuple-element.312), channel_id=1, replica_groups=mesh['section'=4,'row'=2,'col'=4] {'row','col'}, use_global_device_ids=true, to_apply=%region_2.2 | all-reduce | flops 128 | bytes 1024 | tf_op jit(solution)/shard_map/while/body/eval_jaxpr/psum | solution.py:34
  420.2 15.8 %all_gather.53 = bf16[128,2048]{1,0:T(8,128)(2,1)S(1)} all-gather(bf16[128,512]{1,0:T(8,128)(2,1)S(1)} %convert_element_type.72), channel_id=1, replica_groups=mesh['section'=4,'row'=2,'col'=4] {'col'}, dimensions={1}, use_global_device_ids=true | all-gather | bytes 655360 | tf_op jit(solution)/shard_map/while/body/eval_jaxpr/all_gather | solution.py:36
  483.8 28.7 %reduce-scatter.5.cloned.1.call-done = f32[512,128]{0,1:T(8,128)} async-done(((f32[2048,128]{0,1:T(8,128)}), f32[512,128]{0,1:T(8,128)}) %reduce-scatter.5.cloned.1.call-update) | async-done | bytes 262160 | tf_op jit(solution)/shard_map/while/body/eval_jaxpr/reduce_scatter | solution.py:58
  526.4 15.9 %psum.23 = f32[128]{0:T(128)S(1)} all-reduce(f32[128]{0:T(128)S(1)} %get-tuple-element.312), channel_id=1, replica_groups=mesh['section'=4,'row'=2,'col'=4] {'row','col'}, use_global_device_ids=true, to_apply=%region_2.2 | all-reduce | flops 128 | bytes 1024 | tf_op jit(solution)/shard_map/while/body/eval_jaxpr/psum | solution.py:34
  552.7 15.8 %all_gather.53 = bf16[128,2048]{1,0:T(8,128)(2,1)S(1)} all-gather(bf16[128,512]{1,0:T(8,128)(2,1)S(1)} %convert_element_type.72), channel_id=1, replica_groups=mesh['section'=4,'row'=2,'col'=4] {'col'}, dimensions={1}, use_global_device_ids=true | all-gather | bytes 655360 | tf_op jit(solution)/shard_map/while/body/eval_jaxpr/all_gather | solution.py:36
  616.2 28.7 %reduce-scatter.5.cloned.1.call-done = f32[512,128]{0,1:T(8,128)} async-done(((f32[2048,128]{0,1:T(8,128)}), f32[512,128]{0,1:T(8,128)}) %reduce-scatter.5.cloned.1.call-update) | async-done | bytes 262160 | tf_op jit(solution)/shard_map/while/body/eval_jaxpr/reduce_scatter | solution.py:58
  658.8 15.9 %psum.23 = f32[128]{0:T(128)S(1)} all-reduce(f32[128]{0:T(128)S(1)} %get-tuple-element.312), channel_id=1, replica_groups=mesh['section'=4,'row'=2,'col'=4] {'row','col'}, use_global_device_ids=true, to_apply=%region_2.2 | all-reduce | flops 128 | bytes 1024 | tf_op jit(solution)/shard_map/while/body/eval_jaxpr/psum | solution.py:34
  685.1 15.8 %all_gather.53 = bf16[128,2048]{1,0:T(8,128)(2,1)S(1)} all-gather(bf16[128,512]{1,0:T(8,128)(2,1)S(1)} %convert_element_type.72), channel_id=1, replica_groups=mesh['section'=4,'row'=2,'col'=4] {'col'}, dimensions={1}, use_global_device_ids=true | all-gather | bytes 655360 | tf_op jit(solution)/shard_map/while/body/eval_jaxpr/all_gather | solution.py:36
  748.7 28.7 %reduce-scatter.5.cloned.1.call-done = f32[512,128]{0,1:T(8,128)} async-done(((f32[2048,128]{0,1:T(8,128)}), f32[512,128]{0,1:T(8,128)}) %reduce-scatter.5.cloned.1.call-update) | async-done | bytes 262160 | tf_op jit(solution)/shard_map/while/body/eval_jaxpr/reduce_scatter | solution.py:58
  791.3 15.9 %psum.23 = f32[128]{0:T(128)S(1)} all-reduce(f32[128]{0:T(128)S(1)} %get-tuple-element.312), channel_id=1, replica_groups=mesh['section'=4,'row'=2,'col'=4] {'row','col'}, use_global_device_ids=true, to_apply=%region_2.2 | all-reduce | flops 128 | bytes 1024 | tf_op jit(solution)/shard_map/while/body/eval_jaxpr/psum | solution.py:34
  817.6 15.8 %all_gather.53 = bf16[128,2048]{1,0:T(8,128)(2,1)S(1)} all-gather(bf16[128,512]{1,0:T(8,128)(2,1)S(1)} %convert_element_type.72), channel_id=1, replica_groups=mesh['section'=4,'row'=2,'col'=4] {'col'}, dimensions={1}, use_global_device_ids=true | all-gather | bytes 655360 | tf_op jit(solution)/shard_map/while/body/eval_jaxpr/all_gather | solution.py:36
  881.1 28.7 %reduce-scatter.5.cloned.1.call-done = f32[512,128]{0,1:T(8,128)} async-done(((f32[2048,128]{0,1:T(8,128)}), f32[512,128]{0,1:T(8,128)}) %reduce-scatter.5.cloned.1.call-update) | async-done | bytes 262160 | tf_op jit(solution)/shard_map/while/body/eval_jaxpr/reduce_scatter | solution.py:58
  923.7 15.9 %psum.23 = f32[128]{0:T(128)S(1)} all-reduce(f32[128]{0:T(128)S(1)} %get-tuple-element.312), channel_id=1, replica_groups=mesh['section'=4,'row'=2,'col'=4] {'row','col'}, use_global_device_ids=true, to_apply=%region_2.2 | all-reduce | flops 128 | bytes 1024 | tf_op jit(solution)/shard_map/while/body/eval_jaxpr/psum | solution.py:34
  953.1 13.9 %psum.21 = f32[8]{0:T(128)S(1)} all-reduce(f32[8]{0:T(128)S(1)} %fusion.16), channel_id=1, replica_groups=mesh['section'=4,'row'=2,'col'=4] {'row','col'}, use_global_device_ids=true, to_apply=%region_8.9 | all-reduce | flops 8 | bytes 64 | tf_op jit(solution)/shard_map/psum | solution.py:75
  (165 shorter events, 514.6 us)
Async XLA Ops:
  7.2 959.8 %copy-start = (f32[1,8,128,512]{3,2,1,0:T(8,128)S(1)}, f32[1,8,128,512]{3,2,1,0:T(8,128)}, u32[]{:S(2)}) copy-start(f32[1,8,128,512]{3,2,1,0:T(8,128)} %param.14) | copy-start | bytes 6291460
  10.2 48.5 %reduce-scatter.3.cloned.1.call-start = ((), (), s32[]{:S(2)}) async-start(), calls=%async_computation.2 | async-start | bytes 2752512 | tf_op jit(solution)/shard_map/while/body/eval_jaxpr/reduce_scatter | solution.py:40
  10.2 9.9 %collective-permute-start = (f32[128,512]{1,0:T(8,128)}, f32[128,512]{1,0:T(8,128)S(1)}, u32[]{:S(2)}, u32[]{:S(2)}) collective-permute-start(f32[128,512]{1,0:T(8,128)} %get-tuple-element.335), channel_id=1, source_target_pairs={{0,24},{8,0},{16,8},{24,16},{1,25},{9,1},{17,9},{25,17},{2,26},{10... | collective-permute-start | bytes 786440 | tf_op jit(solution)/shard_map/while/body/eval_jaxpr/ppermute | solution.py:12
  46.6 68.5 %reduce-scatter.5.cloned.1.call-start = ((), (), s32[]{:S(2)}) async-start(), calls=%async_computation.3 | async-start | bytes 1310720 | tf_op jit(solution)/shard_map/while/body/eval_jaxpr/reduce_scatter | solution.py:58
  75.4 39.7 %copy-start.2 = (f32[1,512]{1,0:T(1,128)S(1)}, f32[1,512]{1,0:T(1,128)}, u32[]{:S(2)}) copy-start(f32[1,512]{1,0:T(1,128)} %get-tuple-element.357) | copy-start | bytes 6148 | tf_op jit(solution)/shard_map/while
  146.8 44.4 %reduce-scatter.3.cloned.1.call-start = ((), (), s32[]{:S(2)}) async-start(), calls=%async_computation.2 | async-start | bytes 2752512 | tf_op jit(solution)/shard_map/while/body/eval_jaxpr/reduce_scatter | solution.py:40
  146.8 8.6 collective-permute-start
  182.5 65.1 %reduce-scatter.5.cloned.1.call-start = ((), (), s32[]{:S(2)}) async-start(), calls=%async_computation.3 | async-start | bytes 1310720 | tf_op jit(solution)/shard_map/while/body/eval_jaxpr/reduce_scatter | solution.py:58
  279.2 44.4 %reduce-scatter.3.cloned.1.call-start = ((), (), s32[]{:S(2)}) async-start(), calls=%async_computation.2 | async-start | bytes 2752512 | tf_op jit(solution)/shard_map/while/body/eval_jaxpr/reduce_scatter | solution.py:40
  279.2 8.5 collective-permute-start
  314.9 65.1 %reduce-scatter.5.cloned.1.call-start = ((), (), s32[]{:S(2)}) async-start(), calls=%async_computation.3 | async-start | bytes 1310720 | tf_op jit(solution)/shard_map/while/body/eval_jaxpr/reduce_scatter | solution.py:58
  411.7 44.4 %reduce-scatter.3.cloned.1.call-start = ((), (), s32[]{:S(2)}) async-start(), calls=%async_computation.2 | async-start | bytes 2752512 | tf_op jit(solution)/shard_map/while/body/eval_jaxpr/reduce_scatter | solution.py:40
  411.7 8.5 collective-permute-start
  447.4 65.1 %reduce-scatter.5.cloned.1.call-start = ((), (), s32[]{:S(2)}) async-start(), calls=%async_computation.3 | async-start | bytes 1310720 | tf_op jit(solution)/shard_map/while/body/eval_jaxpr/reduce_scatter | solution.py:58
  544.1 44.4 %reduce-scatter.3.cloned.1.call-start = ((), (), s32[]{:S(2)}) async-start(), calls=%async_computation.2 | async-start | bytes 2752512 | tf_op jit(solution)/shard_map/while/body/eval_jaxpr/reduce_scatter | solution.py:40
  544.1 8.5 collective-permute-start
  579.8 65.1 %reduce-scatter.5.cloned.1.call-start = ((), (), s32[]{:S(2)}) async-start(), calls=%async_computation.3 | async-start | bytes 1310720 | tf_op jit(solution)/shard_map/while/body/eval_jaxpr/reduce_scatter | solution.py:58
  676.6 44.4 %reduce-scatter.3.cloned.1.call-start = ((), (), s32[]{:S(2)}) async-start(), calls=%async_computation.2 | async-start | bytes 2752512 | tf_op jit(solution)/shard_map/while/body/eval_jaxpr/reduce_scatter | solution.py:40
  676.6 8.5 collective-permute-start
  712.3 65.1 %reduce-scatter.5.cloned.1.call-start = ((), (), s32[]{:S(2)}) async-start(), calls=%async_computation.3 | async-start | bytes 1310720 | tf_op jit(solution)/shard_map/while/body/eval_jaxpr/reduce_scatter | solution.py:58
  809.0 44.4 %reduce-scatter.3.cloned.1.call-start = ((), (), s32[]{:S(2)}) async-start(), calls=%async_computation.2 | async-start | bytes 2752512 | tf_op jit(solution)/shard_map/while/body/eval_jaxpr/reduce_scatter | solution.py:40
  809.0 8.5 collective-permute-start
  844.7 65.1 %reduce-scatter.5.cloned.1.call-start = ((), (), s32[]{:S(2)}) async-start(), calls=%async_computation.3 | async-start | bytes 1310720 | tf_op jit(solution)/shard_map/while/body/eval_jaxpr/reduce_scatter | solution.py:58
  941.5 8.5 collective-permute-start.1
  (7 other events, 258.6 us)
Sparse Core Ops, SparseCore 0:
  46.7 11.8 reduce-scatter.2
  86.5 28.5 reduce-scatter.4
  182.6 8.5 reduce-scatter.2
  219.0 28.5 reduce-scatter.4
  315.1 8.5 reduce-scatter.2
  351.4 28.5 reduce-scatter.4
  447.5 8.5 reduce-scatter.2
  483.9 28.5 reduce-scatter.4
  580.0 8.5 reduce-scatter.2
  616.3 28.5 reduce-scatter.4
  712.4 8.5 reduce-scatter.2
  748.8 28.5 reduce-scatter.4
  844.8 8.5 reduce-scatter.2
  881.2 28.5 reduce-scatter.4
